TPU v7x, 32 devices: a whole 2x2x4 slice. The times are simulated.
32 devices in a mesh: fsdp: 4 (over x, core), ctx: 4 (over z), tp: 2 (over y).
Axes of the slice: x: 2, y: 2, z: 4, core: 2. Of those that a mesh axis runs over, the one named last changes fastest.
Arguments:
- layer_input: bfloat16 [4096, 2048], P(('fsdp', 'ctx', 'tp')), may hold values from -6 to 6
- cotangent: bfloat16 [4096, 2048], P(('fsdp', 'ctx', 'tp')), may hold values from -6 to 6
- lengths: int32 [4, 2], P('fsdp'), may hold values from 0 to 1024, as said below
- attn_norm: bfloat16 [2048], replicated, may hold values from 0.5 to 1.5
- query_norm_gain: bfloat16 [128], replicated, may hold values from 0.25 to 1.75
- k_norm: bfloat16 [128], replicated, may hold values from 0.25 to 1.75
- w_query: bfloat16 [2048, 2048], P('fsdp', 'tp'), may hold values from -0.125 to 0.125
- key_weight: bfloat16 [2048, 1024], P('fsdp', 'tp'), may hold values from -0.125 to 0.125
- value_weight: bfloat16 [2048, 1024], P('fsdp', 'tp'), may hold values from -0.125 to 0.125
- w_out_gate: bfloat16 [2048, 2048], P('fsdp', 'tp'), may hold values from -0.125 to 0.125
- w_output: bfloat16 [2048, 2048], P(('tp', 'fsdp')), may hold values from -2 to 2
- ffn_norm: bfloat16 [2048], replicated, may hold values from 0.5 to 1.5
- w_gate: bfloat16 [2048, 6144], P('fsdp', 'tp'), may hold values from -0.125 to 0.125
- w_up: bfloat16 [2048, 6144], P('fsdp', 'tp'), may hold values from -0.125 to 0.125
- w_down: bfloat16 [6144, 2048], P(('tp', 'fsdp')), may hold values from -0.078125 to 0.078125
Outputs:
- layer_output: bfloat16 [4096, 2048], P(('fsdp', 'ctx', 'tp'))
- input_grad: bfloat16 [4096, 2048], P(('fsdp', 'ctx', 'tp'))
- grad_attn_norm: float32 [2048], replicated
- grad_q_norm: float32 [128], replicated
- grad_k_norm: float32 [128], replicated
- grad_w_query: float32 [2048, 2048], P('fsdp', 'tp')
- grad_w_key: float32 [2048, 1024], P('fsdp', 'tp')
- grad_w_value: float32 [2048, 1024], P('fsdp', 'tp')
- grad_w_out_gate: float32 [2048, 2048], P('fsdp', 'tp')
- grad_w_output: float32 [2048, 2048], P(('tp', 'fsdp'))
- grad_ffn_norm: float32 [2048], replicated
- grad_w_gate: float32 [2048, 6144], P('fsdp', 'tp')
- grad_w_up: float32 [2048, 6144], P('fsdp', 'tp')
- grad_w_down: float32 [6144, 2048], P(('tp', 'fsdp'))
Inputs may be any that keep to these rules, and one draw needn't show every extreme that they name: `lengths`: per packed row the first count is at least 512 and the two counts add up to at most 1024; some row holds a single sequence of 1024 tokens.
All inputs are finite; a program needn't handle non-finite values.
Results may differ from a plain program's by a relative error of at most 0.024.
Values may be sent and summed in bfloat16 or wider, within the bound.
No kernel may reach another device: no remote copies, remote signals or barrier semaphores. Data moves between devices by JAX's collectives and lax.ppermute only.
A program may use at most 448 MiB of HBM per device.

v0:
```python
import jax
import jax.numpy as jnp
from jax import lax
from jax.sharding import PartitionSpec as P

HEAD_SIZE = 128
EPSILON = 1e-06
ROPE_BASE = 1000000.0
NEG_FILL = -1e30


def as_sent(value):

    def short(part):
        return part.astype(jnp.bfloat16) if part.dtype == jnp.float32 else part

    return jax.tree.map(short, value)


def apply_rms_norm(values, gain_vec):
    return (
        values * lax.rsqrt(jnp.mean(values * values, axis=-1, keepdims=True) + EPSILON) * gain_vec
    )


def norm_back(values, gain_vec, grad_in):
    row_scale = lax.rsqrt(jnp.mean(values * values, axis=-1, keepdims=True) + EPSILON)
    unit_rows = values * row_scale
    scaled = grad_in * gain_vec
    back_rows = row_scale * (
        scaled - unit_rows * jnp.mean(scaled * unit_rows, axis=-1, keepdims=True)
    )
    gain_grad = jnp.sum((grad_in * unit_rows).reshape(-1, values.shape[-1]), axis=0)
    return (back_rows, gain_grad)


def apply_rotary(values, token_position, direction):
    half_size = values.shape[-1] // 2
    frequency = jnp.power(ROPE_BASE, -jnp.arange(half_size, dtype=jnp.float32) / half_size)
    angle = token_position.astype(jnp.float32)[:, None] * frequency[None, :]
    cosine = jnp.cos(angle)[:, None, :]
    sine = direction * jnp.sin(angle)[:, None, :]
    first_half = values[..., :half_size]
    second_half = values[..., half_size:]
    return jnp.concatenate(
        [first_half * cosine - second_half * sine, second_half * cosine + first_half * sine],
        axis=-1,
    )


def segment_of(slot_ids, lengths):
    first_len = lengths[0, 0]
    second_len = lengths[0, 1]
    return jnp.where(slot_ids < first_len, 0, jnp.where(slot_ids < first_len + second_len, 1, 2))


def position_of(slot_ids, segment, lengths):
    seg_begin = jnp.where(
        segment == 0, 0, jnp.where(segment == 1, lengths[0, 0], lengths[0, 0] + lengths[0, 1])
    )
    return slot_ids - seg_begin


def to_block(local_part):
    return lax.all_gather(local_part, "tp", axis=0, tiled=True)


def to_share(partial_rows):
    return lax.psum_scatter(
        partial_rows.astype(jnp.bfloat16), "tp", scatter_dimension=0, tiled=True
    ).astype(jnp.float32)


def fold_product(left_rows, weight_set):
    pieces = jax.tree.map(
        lambda a: lax.all_gather(a, "fsdp", axis=0, tiled=True), as_sent(weight_set)
    )
    return tuple(
        (
            jnp.dot(left_rows, weight_part, preferred_element_type=jnp.float32)
            for weight_part in pieces
        )
    )


def back_product(grad_rows, weight_set):
    pieces = jax.tree.map(
        lambda a: lax.all_gather(a, "fsdp", axis=0, tiled=True), as_sent(weight_set)
    )
    result = lax.dot_general(
        grad_rows[0], pieces[0], (((1,), (1,)), ((), ())), preferred_element_type=jnp.float32
    )
    for grad_part, weight_part in zip(grad_rows[1:], pieces[1:]):
        result = result + lax.dot_general(
            grad_part, weight_part, (((1,), (1,)), ((), ())), preferred_element_type=jnp.float32
        )
    return result


def weight_grads(left_rows, grad_rows):
    widths = [grad_part.shape[1] for grad_part in grad_rows]
    shared = lax.psum_scatter(
        jnp.concatenate(
            [
                lax.dot_general(
                    left_rows,
                    grad_part,
                    (((0,), (0,)), ((), ())),
                    preferred_element_type=jnp.float32,
                )
                for grad_part in grad_rows
            ],
            axis=1,
        ).astype(jnp.bfloat16),
        "fsdp",
        scatter_dimension=0,
        tiled=True,
    )
    summed = lax.psum(shared, "ctx").astype(jnp.float32)
    pieces = []
    offset = 0
    for column_width in widths:
        pieces.append(summed[:, offset : offset + column_width])
        offset = offset + column_width
    return tuple(pieces)


def body(
    layer_input,
    cotangent,
    lengths,
    attn_norm,
    query_norm_gain,
    k_norm,
    w_query,
    key_weight,
    value_weight,
    w_out_gate,
    w_output,
    ffn_norm,
    w_gate,
    w_up,
    w_down,
):
    local_rows = layer_input.shape[0]
    block_rows = local_rows * lax.axis_size("tp")
    query_heads = w_query.shape[1] // HEAD_SIZE
    kv_heads = key_weight.shape[1] // HEAD_SIZE
    groups = query_heads // kv_heads
    score_scale = HEAD_SIZE ** (-0.5)
    block_first = lax.axis_index("ctx") * block_rows
    own_slots = (
        block_first + lax.axis_index("tp") * local_rows + jnp.arange(local_rows, dtype=jnp.int32)
    )
    own_valid = (segment_of(own_slots, lengths) < 2).astype(jnp.float32)[:, None]
    query_slots = block_first + jnp.arange(block_rows, dtype=jnp.int32)
    query_segment = segment_of(query_slots, lengths)
    query_position = position_of(query_slots, query_segment, lengths)
    inputs = layer_input.astype(jnp.float32)
    gain_one = attn_norm.astype(jnp.float32)
    gain_two = ffn_norm.astype(jnp.float32)
    query_gain = query_norm_gain.astype(jnp.float32)
    key_gain = k_norm.astype(jnp.float32)
    first_normed = to_block(apply_rms_norm(inputs, gain_one).astype(jnp.bfloat16))
    query_rows, key_projected, value_proj, gate_logits = fold_product(
        first_normed, (w_query, key_weight, value_weight, w_out_gate)
    )
    query_heads_raw = query_rows.reshape(block_rows, query_heads, HEAD_SIZE)
    key_heads_raw = key_projected.reshape(block_rows, kv_heads, HEAD_SIZE)
    query_rotated = apply_rotary(
        apply_rms_norm(query_heads_raw, query_gain), query_position, 1.0
    ).astype(jnp.bfloat16)
    key_rot = apply_rotary(apply_rms_norm(key_heads_raw, key_gain), query_position, 1.0).astype(
        jnp.bfloat16
    )
    query_grouped = query_rotated.reshape(block_rows, kv_heads, groups, HEAD_SIZE)
    key_flat = key_rot.reshape(block_rows, kv_heads * HEAD_SIZE)
    value_reduced = value_proj.astype(jnp.bfloat16)

    def key_mask(piece_rows):
        key_slots = jnp.arange(piece_rows, dtype=jnp.int32)
        key_segment = segment_of(key_slots, lengths)
        return (query_segment[:, None] == key_segment[None, :]) & (
            key_slots[None, :] <= query_slots[:, None]
        )

    head_shape = (kv_heads, groups, block_rows)
    running_top = jnp.full(head_shape + (1,), NEG_FILL, jnp.float32)
    key_piece = lax.all_gather(key_flat, "ctx", axis=0, tiled=True)
    value_piece = lax.all_gather(value_reduced, "ctx", axis=0, tiled=True)
    piece_rows = key_piece.shape[0]
    allowed = key_mask(piece_rows)
    raw_scores = jnp.einsum(
        "qhgd,khd->hgqk",
        query_grouped,
        key_piece.reshape(piece_rows, kv_heads, HEAD_SIZE),
        preferred_element_type=jnp.float32,
    )
    scores = jnp.where(allowed, raw_scores * score_scale, NEG_FILL)
    new_top = jnp.maximum(running_top, jnp.max(scores, axis=-1, keepdims=True))
    weights = jnp.where(allowed, jnp.exp(scores - new_top), 0.0)
    running_total = jnp.sum(weights, axis=-1, keepdims=True)
    mixed_sum = jnp.einsum(
        "hgqk,khd->hgqd",
        weights.astype(jnp.bfloat16),
        value_piece.reshape(piece_rows, kv_heads, HEAD_SIZE),
        preferred_element_type=jnp.float32,
    )
    mixed_sum, running_top, running_total = (mixed_sum, new_top, running_total)
    log_total = running_top + jnp.log(running_total)
    attended = jnp.transpose(mixed_sum / running_total, (2, 0, 1, 3))
    attended_rows = attended.reshape(block_rows, query_heads * HEAD_SIZE)
    gate_sig = jax.nn.sigmoid(gate_logits)
    gated_mix = (attended_rows * gate_sig).astype(jnp.bfloat16)
    attn_share = to_share(fold_product(gated_mix, (w_output,))[0])
    hidden_in = inputs + own_valid * attn_share
    normed_two = to_block(apply_rms_norm(hidden_in, gain_two).astype(jnp.bfloat16))
    gate_pre, up_pre = fold_product(normed_two, (w_gate, w_up))
    gate_sigmoid = jax.nn.sigmoid(gate_pre)
    activated = gate_pre * gate_sigmoid
    hidden_act = (activated * up_pre).astype(jnp.bfloat16)
    ffn_share = to_share(fold_product(hidden_act, (w_down,))[0])
    layer_output = (hidden_in + own_valid * ffn_share).astype(jnp.bfloat16)
    out_grad = cotangent.astype(jnp.float32) * own_valid
    ffn_grad = to_block(out_grad.astype(jnp.bfloat16))
    hidden_grad = back_product((ffn_grad,), (w_down,))
    grad_w_down = weight_grads(hidden_act, (ffn_grad,))[0]
    gate_grad = (
        hidden_grad * up_pre * gate_sigmoid * (1.0 + gate_pre * (1.0 - gate_sigmoid))
    ).astype(jnp.bfloat16)
    up_grad = (hidden_grad * activated).astype(jnp.bfloat16)
    normed_two_grad = to_share(back_product((gate_grad, up_grad), (w_gate, w_up)))
    grad_w_gate, grad_w_up = weight_grads(normed_two, (gate_grad, up_grad))
    back_two, gain_two_grad = norm_back(hidden_in, gain_two, normed_two_grad)
    hidden_total_grad = out_grad + back_two
    attn_grad = to_block((own_valid * hidden_total_grad).astype(jnp.bfloat16))
    gated_grad = back_product((attn_grad,), (w_output,))
    grad_w_output = weight_grads(gated_mix, (attn_grad,))[0]
    mixed_grad = (gated_grad * gate_sig).astype(jnp.bfloat16)
    gate_logit_grad = (gated_grad * attended_rows * gate_sig * (1.0 - gate_sig)).astype(
        jnp.bfloat16
    )
    mixed_grad_heads = mixed_grad.reshape(block_rows, kv_heads, groups, HEAD_SIZE)
    delta_rows = jnp.transpose(
        jnp.sum(mixed_grad_heads.astype(jnp.float32) * attended, axis=-1), (1, 2, 0)
    )[..., None]
    key_piece = lax.all_gather(key_flat, "ctx", axis=0, tiled=True)
    value_piece = lax.all_gather(value_reduced, "ctx", axis=0, tiled=True)
    piece_rows = key_piece.shape[0]
    key_view = key_piece.reshape(piece_rows, kv_heads, HEAD_SIZE)
    value_view = value_piece.reshape(piece_rows, kv_heads, HEAD_SIZE)
    allowed = key_mask(piece_rows)
    raw_scores = jnp.einsum(
        "qhgd,khd->hgqk", query_grouped, key_view, preferred_element_type=jnp.float32
    )
    soft_vals = jnp.where(allowed, jnp.exp(raw_scores * score_scale - log_total), 0.0)
    prob_grad = jnp.einsum(
        "qhgd,khd->hgqk", mixed_grad_heads, value_view, preferred_element_type=jnp.float32
    )
    score_grad = (soft_vals * (prob_grad - delta_rows) * score_scale).astype(jnp.bfloat16)
    query_acc = jnp.einsum(
        "hgqk,khd->qhgd", score_grad, key_view, preferred_element_type=jnp.float32
    )
    key_part = jnp.einsum(
        "hgqk,qhgd->khd", score_grad, query_grouped, preferred_element_type=jnp.float32
    ).reshape(piece_rows, kv_heads * HEAD_SIZE)
    value_part = jnp.einsum(
        "hgqk,qhgd->khd",
        soft_vals.astype(jnp.bfloat16),
        mixed_grad_heads,
        preferred_element_type=jnp.float32,
    ).reshape(piece_rows, kv_heads * HEAD_SIZE)
    kv_acc = jnp.concatenate([key_part, value_part], axis=1)
    query_acc, kv_acc = (query_acc, kv_acc)
    kv_own = lax.psum_scatter(
        kv_acc.astype(jnp.bfloat16), "ctx", scatter_dimension=0, tiled=True
    ).astype(jnp.float32)
    key_rot_grad = kv_own[:, : kv_heads * HEAD_SIZE].reshape(block_rows, kv_heads, HEAD_SIZE)
    value_grad = kv_own[:, kv_heads * HEAD_SIZE :].astype(jnp.bfloat16)
    key_back, key_gain_grad = norm_back(
        key_heads_raw, key_gain, apply_rotary(key_rot_grad, query_position, -1.0)
    )
    query_back, query_gain_grad = norm_back(
        query_heads_raw,
        query_gain,
        apply_rotary(query_acc.reshape(block_rows, query_heads, HEAD_SIZE), query_position, -1.0),
    )
    query_grad = query_back.reshape(block_rows, query_heads * HEAD_SIZE).astype(jnp.bfloat16)
    key_grad = key_back.reshape(block_rows, kv_heads * HEAD_SIZE).astype(jnp.bfloat16)
    attn_in_grads = (query_grad, key_grad, value_grad, gate_logit_grad)
    normed_one_grad = to_share(
        back_product(attn_in_grads, (w_query, key_weight, value_weight, w_out_gate))
    )
    grad_w_query, grad_w_key, grad_w_value, grad_w_out_gate = weight_grads(
        first_normed, attn_in_grads
    )
    back_one, gain_one_grad = norm_back(inputs, gain_one, normed_one_grad)
    input_grad = (hidden_total_grad + back_one).astype(jnp.bfloat16)
    gain_totals = lax.psum(
        (gain_one_grad, query_gain_grad, key_gain_grad, gain_two_grad), ("fsdp", "ctx", "tp")
    )
    return (
        layer_output,
        input_grad,
        gain_totals[0],
        gain_totals[1],
        gain_totals[2],
        grad_w_query,
        grad_w_key,
        grad_w_value,
        grad_w_out_gate,
        grad_w_output,
        gain_totals[3],
        grad_w_gate,
        grad_w_up,
        grad_w_down,
    )


def solution(mesh):
    return jax.shard_map(
        body,
        mesh=mesh,
        in_specs=(
            P(("fsdp", "ctx", "tp"), None),
            P(("fsdp", "ctx", "tp"), None),
            P("fsdp", None),
            P(),
            P(),
            P(),
            P("fsdp", "tp"),
            P("fsdp", "tp"),
            P("fsdp", "tp"),
            P("fsdp", "tp"),
            P(("tp", "fsdp"), None),
            P(),
            P("fsdp", "tp"),
            P("fsdp", "tp"),
            P(("tp", "fsdp"), None),
        ),
        out_specs=(
            P(("fsdp", "ctx", "tp"), None),
            P(("fsdp", "ctx", "tp"), None),
            P(),
            P(),
            P(),
            P("fsdp", "tp"),
            P("fsdp", "tp"),
            P("fsdp", "tp"),
            P("fsdp", "tp"),
            P(("tp", "fsdp"), None),
            P(),
            P("fsdp", "tp"),
            P("fsdp", "tp"),
            P(("tp", "fsdp"), None),
        ),
        check_vma=False,
    )
```

profile of v0, /device:TPU:0, one launch (start us, length us, event | category | flops | bytes accessed | tf_op | source)
XLA Modules:
  0.0 1699.3 jit_solution(15141842273888128146)
XLA Ops:
  12.8 22.6 %all-gather.15.cloned.1.call-done = bf16[256,2048]{1,0:T(8,128)(2,1)} async-done(((bf16[128,2048]{1,0:T(8,128)(2,1)}), bf16[256,2048]{1,0:T(8,128)(2,1)}) %all-gather.15.cloned.1.call-update) | async-done | bytes 1048592 | tf_op jit(solution)/shard_map/all_gather | solution.py:65
  35.4 24.1 %all-gather.23.cloned.1.call-done = bf16[2048,512]{1,0:T(8,128)(2,1)} async-done(((bf16[512,512]{1,0:T(8,128)(2,1)}), bf16[2048,512]{1,0:T(8,128)(2,1)}) %all-gather.23.cloned.1.call-update) | async-done | bytes 2097168 | tf_op jit(solution)/shard_map/all_gather | solution.py:76
  67.3 16.4 all-gather.17.cloned.1.call-done
  92.2 21.5 %all-gather.25.cloned.1.call-done = bf16[1024,512]{1,0:T(8,128)(2,1)} async-done(((bf16[256,512]{1,0:T(8,128)(2,1)}), bf16[1024,512]{1,0:T(8,128)(2,1)}) %all-gather.25.cloned.1.call-update) | async-done | bytes 1048592 | tf_op jit(solution)/shard_map/all_gather | solution.py:190
  115.9 33.1 %all-gather.21.cloned.1.call-done = bf16[2048,1024]{1,0:T(8,128)(2,1)} async-done(((bf16[512,1024]{1,0:T(8,128)(2,1)}), bf16[2048,1024]{1,0:T(8,128)(2,1)}) %all-gather.21.cloned.1.call-update) | async-done | bytes 4194320 | tf_op jit(solution)/shard_map/all_gather | solution.py:76
  155.1 25.9 %all-gather.19.cloned.1.call-done = bf16[1024,512]{0,1:T(8,128)(2,1)} async-done(((bf16[256,512]{0,1:T(8,128)(2,1)}), bf16[1024,512]{0,1:T(8,128)(2,1)}) %all-gather.19.cloned.1.call-update) | async-done | bytes 1048592 | tf_op jit(solution)/shard_map/all_gather | solution.py:189
  193.8 21.5 %all-gather.27.cloned.1.call-done = bf16[2048,1024]{1,0:T(8,128)(2,1)} async-done(((bf16[512,1024]{1,0:T(8,128)(2,1)}), bf16[2048,1024]{1,0:T(8,128)(2,1)}) %all-gather.27.cloned.1.call-update) | async-done | bytes 4194320 | tf_op jit(solution)/shard_map/all_gather | solution.py:76
  220.3 31.1 %all-gather.29.cloned.1.call-done = bf16[1024,2048]{1,0:T(8,128)(2,1)} async-done(((bf16[256,2048]{1,0:T(8,128)(2,1)}), bf16[1024,2048]{1,0:T(8,128)(2,1)}) %all-gather.29.cloned.1.call-update) | async-done | bytes 4194320 | tf_op jit(solution)/shard_map/all_gather | solution.py:76
  258.0 18.6 %reduce-scatter.10.cloned.1.call-done = bf16[128,2048]{1,0:T(8,128)(2,1)} async-done(((bf16[256,2048]{1,0:T(8,128)(2,1)}), bf16[128,2048]{1,0:T(8,128)(2,1)}) %reduce-scatter.10.cloned.1.call-update) | async-done | bytes 524304 | tf_op jit(solution)/shard_map/reduce_scatter | solution.py:69
  283.6 18.2 %all-gather.31.cloned.1.call-done = bf16[256,2048]{1,0:T(8,128)(2,1)} async-done(((bf16[128,2048]{1,0:T(8,128)(2,1)}), bf16[256,2048]{1,0:T(8,128)(2,1)}) %all-gather.31.cloned.1.call-update) | async-done | bytes 1048592 | tf_op jit(solution)/shard_map/all_gather | solution.py:65
  301.8 83.7 %all-gather.33.cloned.1.call-done = bf16[2048,3072]{1,0:T(8,128)(2,1)} async-done(((bf16[512,3072]{1,0:T(8,128)(2,1)}), bf16[2048,3072]{1,0:T(8,128)(2,1)}) %all-gather.33.cloned.1.call-update) | async-done | bytes 12582928 | tf_op jit(solution)/shard_map/all_gather | solution.py:76
  385.5 10.0 fusion.83
  395.4 73.5 %all-gather.35.cloned.1.call-done = bf16[2048,3072]{1,0:T(8,128)(2,1)} async-done(((bf16[512,3072]{1,0:T(8,128)(2,1)}), bf16[2048,3072]{1,0:T(8,128)(2,1)}) %all-gather.35.cloned.1.call-update) | async-done | bytes 12582928 | tf_op jit(solution)/shard_map/all_gather | solution.py:76
  469.0 10.0 fusion.84
  479.0 13.4 all-gather.39.cloned.1.call-done
  492.4 83.6 %all-gather.37.cloned.1.call-done = bf16[3072,2048]{1,0:T(8,128)(2,1)} async-done(((bf16[768,2048]{1,0:T(8,128)(2,1)}), bf16[3072,2048]{1,0:T(8,128)(2,1)}) %all-gather.37.cloned.1.call-update) | async-done | bytes 12582928 | tf_op jit(solution)/shard_map/all_gather | solution.py:76
  576.0 13.4 multiply_convert_fusion
  596.5 9.1 fusion.20
  605.7 20.5 %reduce-scatter.14.cloned.1.call-done = bf16[128,2048]{1,0:T(8,128)(2,1)} async-done(((bf16[256,2048]{1,0:T(8,128)(2,1)}), bf16[128,2048]{1,0:T(8,128)(2,1)}) %reduce-scatter.14.cloned.1.call-update) | async-done | bytes 524304 | tf_op jit(solution)/shard_map/reduce_scatter | solution.py:69
  632.8 20.1 %all-gather.41.cloned.1.call-done = bf16[256,2048]{1,0:T(8,128)(2,1)} async-done(((bf16[128,2048]{1,0:T(8,128)(2,1)}), bf16[256,2048]{1,0:T(8,128)(2,1)}) %all-gather.41.cloned.1.call-update) | async-done | bytes 1048592 | tf_op jit(solution)/shard_map/all_gather | solution.py:65
  683.2 10.1 convolution_convert_fusion
  734.8 29.6 %pad_maximum_fusion.1 = bf16[2048,3072]{0,1:T(8,128)(2,1)} fusion(bf16[2048,1024]{0,1:T(8,128)(2,1)S(1)} %copy-done.3, bf16[2048,512]{0,1:T(8,128)(2,1)S(1)} %convolution_convert_fusion.6, bf16[2048,512]{0,1:T(8,128)(2,1)S(1)} %convolution_convert_fusion.7, bf16[2048,1024]{0,1:T(8,128)(2,1)S(1)} %copy-done.4), kind=kLoop, calls=%fused_computation.1 | loop fusion | flops 50331648 | bytes 25165824 | tf_op jit(solution)/shard_map/concatenate | solution.py:103
  773.6 8.4 convolution_convert_fusion.2
  782.0 20.1 %pad_maximum_fusion = bf16[2048,6144]{1,0:T(8,128)(2,1)} fusion(bf16[2048,3072]{1,0:T(8,128)(2,1)} %convolution_convert_fusion.1, bf16[2048,3072]{1,0:T(8,128)(2,1)} %convolution_convert_fusion.2), kind=kLoop, calls=%fused_computation | loop fusion | flops 50331648 | bytes 50331648 | tf_op jit(solution)/shard_map/concatenate | solution.py:103
  811.9 9.7 convolution_convert_fusion.9
  821.7 49.5 %reduce-scatter.26.cloned.1.call-done = bf16[768,2048]{1,0:T(8,128)(2,1)} async-done(((bf16[3072,2048]{1,0:T(8,128)(2,1)}), bf16[768,2048]{1,0:T(8,128)(2,1)}) %reduce-scatter.26.cloned.1.call-update) | async-done | bytes 3145744 | tf_op jit(solution)/shard_map/reduce_scatter | solution.py:102
  871.2 99.6 %reduce-scatter.20.cloned.1.call-done = bf16[512,3072]{0,1:T(8,128)(2,1)} async-done(((bf16[2048,3072]{0,1:T(8,128)(2,1)}), bf16[512,3072]{0,1:T(8,128)(2,1)}) %reduce-scatter.20.cloned.1.call-update) | async-done | bytes 3145744 | tf_op jit(solution)/shard_map/reduce_scatter | solution.py:102
  970.8 184.5 %reduce-scatter.24.cloned.1.call-done = bf16[512,6144]{1,0:T(8,128)(2,1)} async-done(((bf16[2048,6144]{1,0:T(8,128)(2,1)}), bf16[512,6144]{1,0:T(8,128)(2,1)}) %reduce-scatter.24.cloned.1.call-update) | async-done | bytes 6291472 | tf_op jit(solution)/shard_map/reduce_scatter | solution.py:102
  1163.6 15.0 reduce-scatter.18.cloned.1.call-done
  1180.1 40.4 %all-reduce = (f32[2048]{0:T(1024)}, f32[128]{0:T(128)}, f32[128]{0:T(128)}, f32[2048]{0:T(1024)}) all-reduce(f32[2048]{0:T(1024)S(1)} %get-tuple-element.44, f32[128]{0:T(128)S(1)} %fusion.51, f32[128]{0:T(128)S(1)} %fusion.62, f32[2048]{0:T(1024)S(1)} %copy-done.46), channel_id=1, replica_groups=mesh['fsdp'=4,'ctx'=4,'tp'=2] {'fsdp','ctx','tp'}, use_global_device_ids=true, to_apply=%region_17.18 | all-reduce | flops 4352 | bytes 34816 | tf_op jit(solution)/shard_map/psum | solution.py:299
  1223.9 440.9 %all-reduce.4.cloned.1.call-done = (bf16[512,3072]{0,1:T(8,128)(2,1)}, bf16[512,6144]{1,0:T(8,128)(2,1)}, bf16[256,2048]{1,0:T(8,128)(2,1)}, bf16[768,2048]{1,0:T(8,128)(2,1)}) async-done(((bf16[512,3072]{0,1:T(8,128)(2,1)}, bf16[512,6144]{1,0:T(8,128)(2,1)}, bf16[256,2048]{1,0:T(8,128)(2,1)}, bf16[768,2048]{1,0:T(8,128)(2,1)}), (bf16[512,3072]{0,1:T(8,128)(2,1)}, bf16[512,6144]{1,0:T(8,128)(2,1)}, ...) | async-done | bytes 13631504 | tf_op jit(solution)/shard_map/psum | solution.py:119
  1679.3 9.4 fusion.75
  (285 shorter events, 195.0 us)
Async XLA Ops:
  7.2 56.4 %copy-start.63 = (bf16[128]{0:T(256)(128)(2,1)S(1)}, bf16[128]{0:T(256)(128)(2,1)}, u32[]{:S(2)}) copy-start(bf16[128]{0:T(256)(128)(2,1)} %param.20) | copy-start | bytes 772
  7.2 56.4 %copy-start.59 = (s32[1,2]{1,0:T(1,128)S(1)}, s32[1,2]{1,0:T(1,128)}, u32[]{:S(2)}) copy-start(s32[1,2]{1,0:T(1,128)} %param.17) | copy-start | bytes 28
  7.2 28.2 %all-gather.15.cloned.1.call-start = ((), (), s32[]{:S(2)}) async-start(), calls=%async_computation.9 | async-start | bytes 1572864 | tf_op jit(solution)/shard_map/all_gather | solution.py:65
  11.2 48.3 %all-gather.23.cloned.1.call-start = ((), (), s32[]{:S(2)}) async-start(), calls=%async_computation.13 | async-start | bytes 2621440 | tf_op jit(solution)/shard_map/all_gather | solution.py:76
  12.0 71.7 %all-gather.17.cloned.1.call-start = ((), (), s32[]{:S(2)}) async-start(), calls=%async_computation.10 | async-start | bytes 2621440 | tf_op jit(solution)/shard_map/all_gather | solution.py:76
  12.7 101.0 %all-gather.25.cloned.1.call-start = ((), (), s32[]{:S(2)}) async-start(), calls=%async_computation.14 | async-start | bytes 1310720 | tf_op jit(solution)/shard_map/all_gather | solution.py:190
  62.9 86.1 %all-gather.21.cloned.1.call-start = ((), (), s32[]{:S(2)}) async-start(), calls=%async_computation.12 | async-start | bytes 5242880 | tf_op jit(solution)/shard_map/all_gather | solution.py:76
  63.5 117.5 %all-gather.19.cloned.1.call-start = ((), (), s32[]{:S(2)}) async-start(), calls=%async_computation.11 | async-start | bytes 1310720 | tf_op jit(solution)/shard_map/all_gather | solution.py:189
  67.3 87.1 %copy-start.27 = (f32[256,64]{1,0:T(8,128)}, f32[256,64]{1,0:T(8,128)S(1)}, u32[]{:S(2)}) copy-start(f32[256,64]{1,0:T(8,128)S(1)} %get-tuple-element.85) | copy-start | bytes 196612
  88.8 126.6 %all-gather.27.cloned.1.call-start = ((), (), s32[]{:S(2)}) async-start(), calls=%async_computation.15 | async-start | bytes 5242880 | tf_op jit(solution)/shard_map/all_gather | solution.py:76
  89.5 161.9 %all-gather.29.cloned.1.call-start = ((), (), s32[]{:S(2)}) async-start(), calls=%async_computation.16 | async-start | bytes 5242880 | tf_op jit(solution)/shard_map/all_gather | solution.py:76
  90.3 186.3 %reduce-scatter.10.cloned.1.call-start = ((), (), s32[]{:S(2)}) async-start(), calls=%async_computation.17 | async-start | bytes 1572864 | tf_op jit(solution)/shard_map/reduce_scatter | solution.py:69
  90.6 63.4 %copy-start.57 = (f32[128]{0:T(128)}, f32[128]{0:T(128)S(1)}, u32[]{:S(2)}) copy-start(f32[128]{0:T(128)S(1)} %convert_element_type.153) | copy-start | bytes 1540
  220.3 56.3 %copy-start.1 = (bf16[128,2048]{1,0:T(8,128)(2,1)S(1)}, bf16[128,2048]{1,0:T(8,128)(2,1)}, u32[]{:S(2)}) copy-start(bf16[128,2048]{1,0:T(8,128)(2,1)} %param.15) | copy-start | bytes 1572868
  256.0 45.8 %all-gather.31.cloned.1.call-start = ((), (), s32[]{:S(2)}) async-start(), calls=%async_computation.18 | async-start | bytes 1572864 | tf_op jit(solution)/shard_map/all_gather | solution.py:65
  280.4 105.1 %all-gather.33.cloned.1.call-start = ((), (), s32[]{:S(2)}) async-start(), calls=%async_computation.19 | async-start | bytes 15728640 | tf_op jit(solution)/shard_map/all_gather | solution.py:76
  281.1 187.9 %all-gather.35.cloned.1.call-start = ((), (), s32[]{:S(2)}) async-start(), calls=%async_computation.20 | async-start | bytes 15728640 | tf_op jit(solution)/shard_map/all_gather | solution.py:76
  281.7 210.7 %all-gather.39.cloned.1.call-start = ((), (), s32[]{:S(2)}) async-start(), calls=%async_computation.23 | async-start | bytes 1572864 | tf_op jit(solution)/shard_map/all_gather | solution.py:65
  282.4 293.6 %all-gather.37.cloned.1.call-start = ((), (), s32[]{:S(2)}) async-start(), calls=%async_computation.21 | async-start | bytes 15728640 | tf_op jit(solution)/shard_map/all_gather | solution.py:76
  283.0 343.2 %reduce-scatter.14.cloned.1.call-start = ((), (), s32[]{:S(2)}) async-start(), calls=%async_computation.24 | async-start | bytes 1572864 | tf_op jit(solution)/shard_map/reduce_scatter | solution.py:69
  605.6 47.3 %all-gather.41.cloned.1.call-start = ((), (), s32[]{:S(2)}) async-start(), calls=%async_computation.25 | async-start | bytes 1572864 | tf_op jit(solution)/shard_map/all_gather | solution.py:65
  631.5 90.7 %reduce-scatter.16.cloned.1.call-start = ((), (), s32[]{:S(2)}) async-start(), calls=%async_computation.26 | async-start | bytes 2621440 | tf_op jit(solution)/shard_map/reduce_scatter | solution.py:275
  678.4 143.3 %reduce-scatter.22.cloned.1.call-start = ((), (), s32[]{:S(2)}) async-start(), calls=%async_computation.29 | async-start | bytes 5242880 | tf_op jit(solution)/shard_map/reduce_scatter | solution.py:102
  683.1 188.0 %reduce-scatter.26.cloned.1.call-start = ((), (), s32[]{:S(2)}) async-start(), calls=%async_computation.31 | async-start | bytes 15728640 | tf_op jit(solution)/shard_map/reduce_scatter | solution.py:102
  693.3 277.5 %reduce-scatter.20.cloned.1.call-start = ((), (), s32[]{:S(2)}) async-start(), calls=%async_computation.28 | async-start | bytes 15728640 | tf_op jit(solution)/shard_map/reduce_scatter | solution.py:102
  764.4 390.9 %reduce-scatter.24.cloned.1.call-start = ((), (), s32[]{:S(2)}) async-start(), calls=%async_computation.30 | async-start | bytes 31457280 | tf_op jit(solution)/shard_map/reduce_scatter | solution.py:102
  802.1 376.5 %reduce-scatter.18.cloned.1.call-start = ((), (), s32[]{:S(2)}) async-start(), calls=%async_computation.27 | async-start | bytes 1572864 | tf_op jit(solution)/shard_map/reduce_scatter | solution.py:69
  811.8 408.6 %reduce-scatter.12.cloned.1.call-start = ((), (), s32[]{:S(2)}) async-start(), calls=%async_computation.22 | async-start | bytes 1572864 | tf_op jit(solution)/shard_map/reduce_scatter | solution.py:69
  821.6 843.2 %all-reduce.4.cloned.1.call-start = ((), (), s32[]{:S(2)}) async-start(), calls=%async_computation.32 | async-start | bytes 27262976 | tf_op jit(solution)/shard_map/psum | solution.py:119
  1157.4 63.1 %copy-start.48 = (f32[128]{0:T(128)S(1)}, f32[128]{0:T(128)}, u32[]{:S(2)}) copy-start(f32[128]{0:T(128)} %compare_convert_fusion) | copy-start | bytes 1540
  1157.4 63.1 %copy-start.51 = (f32[128]{0:T(128)S(1)}, f32[128]{0:T(128)}, u32[]{:S(2)}) copy-start(f32[128]{0:T(128)} %copy-done.50) | copy-start | bytes 1540
  1157.4 63.1 %copy-start.61 = (f32[128]{0:T(128)S(1)}, f32[128]{0:T(128)}, u32[]{:S(2)}) copy-start(f32[128]{0:T(128)} %copy-done.60) | copy-start | bytes 1540
  (57 other events, 487.8 us)
Sparse Core Ops, SparseCore 0:
  11.4 23.9 all-gather.14
  37.0 22.5 all-gather.22
  61.1 22.5 all-gather.16
  85.7 27.9 all-gather.24
  115.2 33.8 all-gather.20
  151.0 29.9 all-gather.18
  182.5 32.7 all-gather.26
  216.9 34.4 all-gather.28
  256.1 20.3 reduce-scatter.9
  280.5 21.2 all-gather.30
  303.4 82.0 all-gather.32
  386.9 82.0 all-gather.34
  471.1 21.2 all-gather.38
  493.8 82.1 all-gather.36
  605.7 20.3 reduce-scatter.13
  631.6 21.2 all-gather.40
  678.5 43.6 reduce-scatter.15
  725.1 43.7 reduce-scatter.21
  771.5 99.6 reduce-scatter.25
  873.6 97.1 reduce-scatter.19
  973.4 181.8 reduce-scatter.23
  1158.1 20.3 reduce-scatter.17
  1181.4 20.5 reduce-scatter.11
  1204.8 459.9 all-reduce.3
where the time goes:
time: 1700 us
  waiting for transfers between devices  1330 us (78%)
  matrix products  153 us (9%)
  other arithmetic  98.6 us (6%)
  local copies, waits for them, and re-layouts  58.1 us (3%)
  blocking collectives  40.4 us (2%)
    psum x1, waiting for transfers between devices, weight_grads(): summed = lax.psum(shared, 'ctx').astype(jnp.float32)  441 us
    all_gather x8, waiting for transfers between devices, fold_product(): lax.all_gather(a, 'fsdp', axis=0, tiled=True)  367 us
    reduce_scatter x4, waiting for transfers between devices, weight_grads(): lax.psum_scatter(jnp.concatenate([lax.dot_general(left_rows, grad_part, (...  334 us
    all_gather x4, waiting for transfers between devices, to_block(): return lax.all_gather(local_part, 'tp', axis=0, tiled=True)  74.3 us
    reduce_scatter x4, waiting for transfers between devices, to_share(): lax.psum_scatter(partial_rows.astype(jnp.bfloat16), 'tp', scatter_dimensi...  54.1 us
    concatenate x2, other arithmetic, weight_grads(): jnp.concatenate([lax.dot_general(left_rows, grad_part, (((0,), (0,)), (()...  49.7 us
    dot_general x8, matrix products, fold_product(): jnp.dot(left_rows, weight_part, preferred_element_type=jnp.float32)  48.3 us
    psum x1, blocking collectives, body(): lax.psum((gain_one_grad, query_gain_grad, key_gain_grad, gain_two_grad),...  40.4 us
  transfers between devices with their start and end apart: 24, of which 22 were waited for; matrix products, arithmetic and copies ran while one was open for 12% of the time, Pallas kernels for 0%

commit v1 on v0

--- a/solution.py
+++ b/solution.py
@@ -116,7 +116,7 @@
         scatter_dimension=0,
         tiled=True,
     )
-    summed = lax.psum(shared, "ctx").astype(jnp.float32)
+    summed = jnp.sum(lax.all_gather(shared, "ctx"), axis=0).astype(jnp.float32)
     pieces = []
     offset = 0
     for column_width in widths:

time: 1700 us -> 2190 us (1.29)
  waiting for transfers between devices: 1330 us -> 1740 us
  other arithmetic: 98.6 us -> 148 us
  local copies, waits for them, and re-layouts: 58.1 us -> 81.9 us
    all_gather x0 -> x4, waiting for transfers between devices: none -> 848 us  [weight_grads(): summed = jnp.sum(lax.all_gather(shared, 'ctx'), axis=0).astype(jnp.float32)]
    psum x1 -> x0, waiting for transfers between devices: 441 us -> none  [weight_grads(): summed = lax.psum(shared, 'ctx').astype(jnp.float32)]
    reduce_sum x0 -> x4, other arithmetic: none -> 49.5 us  [weight_grads(): summed = jnp.sum(lax.all_gather(shared, 'ctx'), axis=0).astype(jnp.float32)]
    all_gather x0 -> x1, local copies, waits for them, and re-layouts: none -> 22 us  [weight_grads(): summed = jnp.sum(lax.all_gather(shared, 'ctx'), axis=0).astype(jnp.float32)]
  transfers between devices with their start and end apart: 24 -> 27, of which waited for: 22 -> 25; matrix products, arithmetic and copies ran while one was open for 12% -> 13% of each run, Pallas kernels for 0% -> 0%
where the time goes in v1:
time: 2190 us; the launch traced here: 2180 us
  waiting for transfers between devices  1740 us (79%)
  matrix products  152 us (7%)
  other arithmetic  148 us (7%)
  local copies, waits for them, and re-layouts  81.9 us (4%)
  blocking collectives  40.3 us (2%)
    all_gather x4, waiting for transfers between devices, weight_grads(): summed = jnp.sum(lax.all_gather(shared, 'ctx'), axis=0).astype(jnp.float32)  848 us
    all_gather x8, waiting for transfers between devices, fold_product(): lax.all_gather(a, 'fsdp', axis=0, tiled=True)  367 us
    reduce_scatter x4, waiting for transfers between devices, weight_grads(): lax.psum_scatter(jnp.concatenate([lax.dot_general(left_rows, grad_part, (...  333 us
    all_gather x4, waiting for transfers between devices, to_block(): return lax.all_gather(local_part, 'tp', axis=0, tiled=True)  74.7 us
    reduce_scatter x4, waiting for transfers between devices, to_share(): lax.psum_scatter(partial_rows.astype(jnp.bfloat16), 'tp', scatter_dimensi...  54.2 us
    concatenate x2, other arithmetic, weight_grads(): jnp.concatenate([lax.dot_general(left_rows, grad_part, (((0,), (0,)), (()...  49.8 us
    reduce_sum x4, other arithmetic, weight_grads(): summed = jnp.sum(lax.all_gather(shared, 'ctx'), axis=0).astype(jnp.float32)  49.5 us
    dot_general x8, matrix products, fold_product(): jnp.dot(left_rows, weight_part, preferred_element_type=jnp.float32)  48.3 us
  transfers between devices with their start and end apart: 27, of which 25 were waited for; matrix products, arithmetic and copies ran while one was open for 13% of the time, Pallas kernels for 0%

profile of v1, /device:TPU:0, one launch (start us, length us, event | category | flops | bytes accessed | tf_op | source)
XLA Modules:
  0.0 2179.9 jit_solution(6096626165355810287)
XLA Ops:
  13.3 22.6 %all-gather.23.cloned.1.call-done = bf16[256,2048]{1,0:T(8,128)(2,1)} async-done(((bf16[128,2048]{1,0:T(8,128)(2,1)}), bf16[256,2048]{1,0:T(8,128)(2,1)}) %all-gather.23.cloned.1.call-update) | async-done | bytes 1048592 | tf_op jit(solution)/shard_map/all_gather | solution.py:65
  36.0 24.1 %all-gather.31.cloned.1.call-done = bf16[2048,512]{1,0:T(8,128)(2,1)} async-done(((bf16[512,512]{1,0:T(8,128)(2,1)}), bf16[2048,512]{1,0:T(8,128)(2,1)}) %all-gather.31.cloned.1.call-update) | async-done | bytes 2097168 | tf_op jit(solution)/shard_map/all_gather | solution.py:76
  67.9 16.4 all-gather.25.cloned.1.call-done
  93.0 21.3 all-gather.33.cloned.1.call-done
  116.5 33.1 %all-gather.29.cloned.1.call-done = bf16[2048,1024]{1,0:T(8,128)(2,1)} async-done(((bf16[512,1024]{1,0:T(8,128)(2,1)}), bf16[2048,1024]{1,0:T(8,128)(2,1)}) %all-gather.29.cloned.1.call-update) | async-done | bytes 4194320 | tf_op jit(solution)/shard_map/all_gather | solution.py:76
  155.7 25.8 %all-gather.27.cloned.1.call-done = bf16[1024,512]{0,1:T(8,128)(2,1)} async-done(((bf16[256,512]{0,1:T(8,128)(2,1)}), bf16[1024,512]{0,1:T(8,128)(2,1)}) %all-gather.27.cloned.1.call-update) | async-done | bytes 1048592 | tf_op jit(solution)/shard_map/all_gather | solution.py:189
  194.4 21.5 all-gather.35.cloned.1.call-done
  220.9 31.1 %all-gather.37.cloned.1.call-done = bf16[1024,2048]{1,0:T(8,128)(2,1)} async-done(((bf16[256,2048]{1,0:T(8,128)(2,1)}), bf16[1024,2048]{1,0:T(8,128)(2,1)}) %all-gather.37.cloned.1.call-update) | async-done | bytes 4194320 | tf_op jit(solution)/shard_map/all_gather | solution.py:76
  258.5 18.6 reduce-scatter.10.cloned.1.call-done
  283.8 18.6 all-gather.39.cloned.1.call-done
  302.4 83.7 %all-gather.41.cloned.1.call-done = bf16[2048,3072]{1,0:T(8,128)(2,1)} async-done(((bf16[512,3072]{1,0:T(8,128)(2,1)}), bf16[2048,3072]{1,0:T(8,128)(2,1)}) %all-gather.41.cloned.1.call-update) | async-done | bytes 12582928 | tf_op jit(solution)/shard_map/all_gather | solution.py:76
  396.0 73.5 %all-gather.43.cloned.1.call-done = bf16[2048,3072]{1,0:T(8,128)(2,1)} async-done(((bf16[512,3072]{1,0:T(8,128)(2,1)}), bf16[2048,3072]{1,0:T(8,128)(2,1)}) %all-gather.43.cloned.1.call-update) | async-done | bytes 12582928 | tf_op jit(solution)/shard_map/all_gather | solution.py:76
  479.6 13.4 all-gather.47.cloned.1.call-done
  493.0 83.5 %all-gather.45.cloned.1.call-done = bf16[3072,2048]{1,0:T(8,128)(2,1)} async-done(((bf16[768,2048]{1,0:T(8,128)(2,1)}), bf16[3072,2048]{1,0:T(8,128)(2,1)}) %all-gather.45.cloned.1.call-update) | async-done | bytes 12582928 | tf_op jit(solution)/shard_map/all_gather | solution.py:76
  576.6 13.4 multiply_convert_fusion
  606.3 20.5 reduce-scatter.14.cloned.1.call-done
  633.5 20.1 all-gather.49.cloned.1.call-done
  684.0 10.1 convolution_convert_fusion
  735.6 29.4 %pad_maximum_fusion.1 = bf16[2048,3072]{0,1:T(8,128)(2,1)} fusion(bf16[2048,1024]{0,1:T(8,128)(2,1)S(1)} %copy-done.3, bf16[2048,512]{0,1:T(8,128)(2,1)S(1)} %convolution_convert_fusion.6, bf16[2048,512]{0,1:T(8,128)(2,1)S(1)} %convolution_convert_fusion.7, bf16[2048,1024]{0,1:T(8,128)(2,1)S(1)} %copy-done.4), kind=kLoop, calls=%fused_computation.1 | loop fusion | flops 50331648 | bytes 25165824 | tf_op jit(solution)/shard_map/concatenate | solution.py:103
  782.3 20.4 pad_maximum_fusion
  823.0 49.0 %reduce-scatter.26.cloned.1.call-done = bf16[768,2048]{1,0:T(8,128)(2,1)} async-done(((bf16[3072,2048]{1,0:T(8,128)(2,1)}), bf16[768,2048]{1,0:T(8,128)(2,1)}) %reduce-scatter.26.cloned.1.call-update) | async-done | bytes 3145744 | tf_op jit(solution)/shard_map/reduce_scatter | solution.py:102
  872.0 99.6 %reduce-scatter.20.cloned.1.call-done = bf16[512,3072]{0,1:T(8,128)(2,1)} async-done(((bf16[2048,3072]{0,1:T(8,128)(2,1)}), bf16[512,3072]{0,1:T(8,128)(2,1)}) %reduce-scatter.20.cloned.1.call-update) | async-done | bytes 3145744 | tf_op jit(solution)/shard_map/reduce_scatter | solution.py:102
  971.6 184.5 %reduce-scatter.24.cloned.1.call-done = bf16[512,6144]{1,0:T(8,128)(2,1)} async-done(((bf16[2048,6144]{1,0:T(8,128)(2,1)}), bf16[512,6144]{1,0:T(8,128)(2,1)}) %reduce-scatter.24.cloned.1.call-update) | async-done | bytes 6291472 | tf_op jit(solution)/shard_map/reduce_scatter | solution.py:102
  1164.3 15.0 reduce-scatter.18.cloned.1.call-done
  1180.8 40.3 %all-reduce = (f32[2048]{0:T(1024)}, f32[128]{0:T(128)}, f32[128]{0:T(128)}, f32[2048]{0:T(1024)}) all-reduce(f32[2048]{0:T(1024)S(1)} %get-tuple-element.30, f32[128]{0:T(128)S(1)} %fusion.51, f32[128]{0:T(128)S(1)} %fusion.62, f32[2048]{0:T(1024)S(1)} %copy-done.46), channel_id=1, replica_groups=mesh['fsdp'=4,'ctx'=4,'tp'=2] {'fsdp','ctx','tp'}, use_global_device_ids=true, to_apply=%region_17.18 | all-reduce | flops 4352 | bytes 34816 | tf_op jit(solution)/shard_map/psum | solution.py:299
  1224.6 60.4 %all-gather.53.cloned.1.call-done = bf16[1024,2048]{1,0:T(8,128)(2,1)} async-done(((bf16[256,2048]{1,0:T(8,128)(2,1)}), bf16[1024,2048]{1,0:T(8,128)(2,1)}) %all-gather.53.cloned.1.call-update) | async-done | bytes 4194320 | tf_op jit(solution)/shard_map/all_gather | solution.py:119
  1289.6 213.6 %all-gather.57.cloned.1.call-done = bf16[3072,2048]{1,0:T(8,128)(2,1)} async-done(((bf16[768,2048]{1,0:T(8,128)(2,1)}), bf16[3072,2048]{1,0:T(8,128)(2,1)}) %all-gather.57.cloned.1.call-update) | async-done | bytes 12582928 | tf_op jit(solution)/shard_map/all_gather | solution.py:119
  1515.8 205.3 %all-gather.51.cloned.1.call-done = bf16[2048,3072]{0,1:T(8,128)(2,1)} async-done(((bf16[512,3072]{0,1:T(8,128)(2,1)}), bf16[2048,3072]{0,1:T(8,128)(2,1)}) %all-gather.51.cloned.1.call-update) | async-done | bytes 12582928 | tf_op jit(solution)/shard_map/all_gather | solution.py:119
  1721.1 22.0 %reshape.307 = bf16[4,512,3072]{1,0,2:T(4,128)(2,1)} reshape(bf16[2048,3072]{0,1:T(8,128)(2,1)} %all-gather.51.cloned.1.call-done) | data formatting | bytes 25165824 | tf_op jit(solution)/shard_map/all_gather | solution.py:119
  1743.1 19.9 reduce_sum.203
  1777.3 368.6 %all-gather.55.cloned.1.call-done = bf16[2048,6144]{1,0:T(8,128)(2,1)} async-done(((bf16[512,6144]{1,0:T(8,128)(2,1)}), bf16[2048,6144]{1,0:T(8,128)(2,1)}) %all-gather.55.cloned.1.call-update) | async-done | bytes 25165840 | tf_op jit(solution)/shard_map/all_gather | solution.py:119
  2145.9 17.7 reduce_sum.206
  (299 shorter events, 265.9 us)
Async XLA Ops:
  7.2 28.8 %all-gather.23.cloned.1.call-start = ((), (), s32[]{:S(2)}) async-start(), calls=%async_computation.9 | async-start | bytes 1572864 | tf_op jit(solution)/shard_map/all_gather | solution.py:65
  11.8 48.3 %all-gather.31.cloned.1.call-start = ((), (), s32[]{:S(2)}) async-start(), calls=%async_computation.13 | async-start | bytes 2621440 | tf_op jit(solution)/shard_map/all_gather | solution.py:76
  12.6 71.7 %all-gather.25.cloned.1.call-start = ((), (), s32[]{:S(2)}) async-start(), calls=%async_computation.10 | async-start | bytes 2621440 | tf_op jit(solution)/shard_map/all_gather | solution.py:76
  13.3 101.0 %all-gather.33.cloned.1.call-start = ((), (), s32[]{:S(2)}) async-start(), calls=%async_computation.14 | async-start | bytes 1310720 | tf_op jit(solution)/shard_map/all_gather | solution.py:190
  63.5 86.1 %all-gather.29.cloned.1.call-start = ((), (), s32[]{:S(2)}) async-start(), calls=%async_computation.12 | async-start | bytes 5242880 | tf_op jit(solution)/shard_map/all_gather | solution.py:76
  64.1 117.5 %all-gather.27.cloned.1.call-start = ((), (), s32[]{:S(2)}) async-start(), calls=%async_computation.11 | async-start | bytes 1310720 | tf_op jit(solution)/shard_map/all_gather | solution.py:189
  67.9 87.1 %copy-start.27 = (f32[256,64]{1,0:T(8,128)}, f32[256,64]{1,0:T(8,128)S(1)}, u32[]{:S(2)}) copy-start(f32[256,64]{1,0:T(8,128)S(1)} %get-tuple-element.67) | copy-start | bytes 196612
  89.3 126.6 %all-gather.35.cloned.1.call-start = ((), (), s32[]{:S(2)}) async-start(), calls=%async_computation.15 | async-start | bytes 5242880 | tf_op jit(solution)/shard_map/all_gather | solution.py:76
  90.1 161.9 %all-gather.37.cloned.1.call-start = ((), (), s32[]{:S(2)}) async-start(), calls=%async_computation.16 | async-start | bytes 5242880 | tf_op jit(solution)/shard_map/all_gather | solution.py:76
  90.8 186.3 %reduce-scatter.10.cloned.1.call-start = ((), (), s32[]{:S(2)}) async-start(), calls=%async_computation.17 | async-start | bytes 1572864 | tf_op jit(solution)/shard_map/reduce_scatter | solution.py:69
  91.4 63.2 %copy-start.57 = (f32[128]{0:T(128)}, f32[128]{0:T(128)S(1)}, u32[]{:S(2)}) copy-start(f32[128]{0:T(128)S(1)} %convert_element_type.161) | copy-start | bytes 1540
  256.6 45.8 %all-gather.39.cloned.1.call-start = ((), (), s32[]{:S(2)}) async-start(), calls=%async_computation.18 | async-start | bytes 1572864 | tf_op jit(solution)/shard_map/all_gather | solution.py:65
  280.9 105.1 %all-gather.41.cloned.1.call-start = ((), (), s32[]{:S(2)}) async-start(), calls=%async_computation.19 | async-start | bytes 15728640 | tf_op jit(solution)/shard_map/all_gather | solution.py:76
  281.7 187.9 %all-gather.43.cloned.1.call-start = ((), (), s32[]{:S(2)}) async-start(), calls=%async_computation.20 | async-start | bytes 15728640 | tf_op jit(solution)/shard_map/all_gather | solution.py:76
  282.3 210.7 %all-gather.47.cloned.1.call-start = ((), (), s32[]{:S(2)}) async-start(), calls=%async_computation.23 | async-start | bytes 1572864 | tf_op jit(solution)/shard_map/all_gather | solution.py:65
  283.0 293.5 %all-gather.45.cloned.1.call-start = ((), (), s32[]{:S(2)}) async-start(), calls=%async_computation.21 | async-start | bytes 15728640 | tf_op jit(solution)/shard_map/all_gather | solution.py:76
  283.6 343.2 %reduce-scatter.14.cloned.1.call-start = ((), (), s32[]{:S(2)}) async-start(), calls=%async_computation.24 | async-start | bytes 1572864 | tf_op jit(solution)/shard_map/reduce_scatter | solution.py:69
  606.3 47.3 %all-gather.49.cloned.1.call-start = ((), (), s32[]{:S(2)}) async-start(), calls=%async_computation.25 | async-start | bytes 1572864 | tf_op jit(solution)/shard_map/all_gather | solution.py:65
  632.2 90.8 %reduce-scatter.16.cloned.1.call-start = ((), (), s32[]{:S(2)}) async-start(), calls=%async_computation.26 | async-start | bytes 2621440 | tf_op jit(solution)/shard_map/reduce_scatter | solution.py:275
  679.2 143.3 %reduce-scatter.22.cloned.1.call-start = ((), (), s32[]{:S(2)}) async-start(), calls=%async_computation.29 | async-start | bytes 5242880 | tf_op jit(solution)/shard_map/reduce_scatter | solution.py:102
  683.9 188.0 %reduce-scatter.26.cloned.1.call-start = ((), (), s32[]{:S(2)}) async-start(), calls=%async_computation.31 | async-start | bytes 15728640 | tf_op jit(solution)/shard_map/reduce_scatter | solution.py:102
  694.1 277.5 %reduce-scatter.20.cloned.1.call-start = ((), (), s32[]{:S(2)}) async-start(), calls=%async_computation.28 | async-start | bytes 15728640 | tf_op jit(solution)/shard_map/reduce_scatter | solution.py:102
  765.0 391.1 %reduce-scatter.24.cloned.1.call-start = ((), (), s32[]{:S(2)}) async-start(), calls=%async_computation.30 | async-start | bytes 31457280 | tf_op jit(solution)/shard_map/reduce_scatter | solution.py:102
  802.7 376.6 %reduce-scatter.18.cloned.1.call-start = ((), (), s32[]{:S(2)}) async-start(), calls=%async_computation.27 | async-start | bytes 1572864 | tf_op jit(solution)/shard_map/reduce_scatter | solution.py:69
  812.6 408.6 %reduce-scatter.12.cloned.1.call-start = ((), (), s32[]{:S(2)}) async-start(), calls=%async_computation.22 | async-start | bytes 1572864 | tf_op jit(solution)/shard_map/reduce_scatter | solution.py:69
  822.4 462.6 %all-gather.53.cloned.1.call-start = ((), (), s32[]{:S(2)}) async-start(), calls=%async_computation.33 | async-start | bytes 5242880 | tf_op jit(solution)/shard_map/all_gather | solution.py:119
  822.9 680.3 %all-gather.57.cloned.1.call-start = ((), (), s32[]{:S(2)}) async-start(), calls=%async_computation.35 | async-start | bytes 15728640 | tf_op jit(solution)/shard_map/all_gather | solution.py:119
  872.0 849.1 %all-gather.51.cloned.1.call-start = ((), (), s32[]{:S(2)}) async-start(), calls=%async_computation.32 | async-start | bytes 15728640 | tf_op jit(solution)/shard_map/all_gather | solution.py:119
  971.6 1174.3 %all-gather.55.cloned.1.call-start = ((), (), s32[]{:S(2)}) async-start(), calls=%async_computation.34 | async-start | bytes 31457280 | tf_op jit(solution)/shard_map/all_gather | solution.py:119
  1158.2 63.0 %copy-start.48 = (f32[128]{0:T(128)S(1)}, f32[128]{0:T(128)}, u32[]{:S(2)}) copy-start(f32[128]{0:T(128)} %compare_convert_fusion) | copy-start | bytes 1540
  1158.2 63.0 %copy-start.51 = (f32[128]{0:T(128)S(1)}, f32[128]{0:T(128)}, u32[]{:S(2)}) copy-start(f32[128]{0:T(128)} %copy-done.50) | copy-start | bytes 1540
  1158.2 63.0 %copy-start.61 = (f32[128]{0:T(128)S(1)}, f32[128]{0:T(128)}, u32[]{:S(2)}) copy-start(f32[128]{0:T(128)} %copy-done.60) | copy-start | bytes 1540
  (60 other events, 673.4 us)
Sparse Core Ops, SparseCore 0:
  11.9 23.9 all-gather.22
  37.5 22.5 all-gather.30
  61.7 22.5 all-gather.24
  86.3 27.9 all-gather.32
  115.7 33.8 all-gather.28
  151.6 29.9 all-gather.26
  183.1 32.7 all-gather.34
  217.5 34.4 all-gather.36
  256.7 20.3 reduce-scatter.9
  281.1 21.2 all-gather.38
  303.9 82.0 all-gather.40
  387.4 82.0 all-gather.42
  471.7 21.2 all-gather.46
  494.4 82.0 all-gather.44
  606.4 20.3 reduce-scatter.13
  632.3 21.2 all-gather.48
  679.3 43.5 reduce-scatter.15
  725.9 43.7 reduce-scatter.21
  772.3 99.6 reduce-scatter.25
  874.4 97.1 reduce-scatter.19
  974.2 181.8 reduce-scatter.23
  1158.9 20.3 reduce-scatter.17
  1182.2 20.5 reduce-scatter.11
  1204.3 80.6 all-gather.52
  1286.5 216.6 all-gather.56
  1504.7 216.3 all-gather.50
  1722.5 423.3 all-gather.54
